TPU v7x, 32 devices: a whole 2x2x4 slice. The times are simulated.
32 devices in a mesh: row: 8 (over y, x, core), col: 4 (over z).
Axes of the slice: x: 2, y: 2, z: 4, core: 2. Of those that a mesh axis runs over, the one named last changes fastest.
Arguments:
- shear_stress: float32 [512, 16384], P(None, ('row', 'col')), may hold values from -3.5 to 3.5
- state_var: float32 [512, 16384], P(None, ('row', 'col')), may hold values from -0.4 to 0.4
- a_param: float32 [16384], P(('row', 'col')), may hold values from 0.7 to 1.4
- rate_param: float32 [16384], P(('row', 'col')), may hold values from 0.1 to 0.5
- loading: float32 [16384], P(('row', 'col')), may hold values from 0.1 to 1
- dense_tiles: bfloat16 [16384, 16384], P('row', 'col'), may hold values from -0.046875 to 0.046875
- left_factor: bfloat16 [512, 16384], P('col', 'row'), may hold values from -0.75 to 0.75
- right_factor: bfloat16 [512, 16384], P('row', 'col'), may hold values from -0.046875 to 0.046875
- admissible: int32 [8, 8], replicated, may hold values from 0 to 1, as said below
- tile_ranks: int32 [8, 8], replicated, may hold values from 16 to 64
Outputs:
- shear_next: float32 [512, 16384], P(None, ('row', 'col'))
- state_next: float32 [512, 16384], P(None, ('row', 'col'))
Inputs may be any that keep to these rules, and one draw needn't show every extreme that they name: `admissible`: tiles on the diagonal and next to it are always dense; elsewhere a tile is dense or low-rank at random.
All inputs are finite; a program needn't handle non-finite values.
Results may differ from a plain program's by a relative error of at most 0.0024.
Values may be sent and summed in bfloat16 or wider, within the bound.
A program may use at most 128 MiB of HBM per device.

v0:
```python
import jax
import jax.numpy as jnp
from jax import lax
from jax.sharding import PartitionSpec as P

TILE = 2048
RANK = 64


def slip_velocity(shear_now, state_now, a_param):
    return jnp.sinh(shear_now / a_param[None, :]) * jnp.exp(-state_now)


def tile_product(vec_tile, dense_tile, left_tile, right_tile, is_dense, rank_here):

    def dense_branch(operands):
        return lax.dot_general(
            operands[0], operands[1], (((1,), (1,)), ((), ())), preferred_element_type=jnp.float32
        )

    def factor_branch(operands):
        projection = lax.dot_general(
            operands[0], operands[3], (((1,), (1,)), ((), ())), preferred_element_type=jnp.float32
        )
        keep_mask = jnp.arange(projection.shape[1], dtype=jnp.int32)[None, :] < rank_here
        projection = jnp.where(keep_mask, projection, jnp.zeros_like(projection)).astype(
            jnp.bfloat16
        )
        return jnp.dot(projection, operands[2], preferred_element_type=jnp.float32)

    return lax.cond(
        is_dense == 1, dense_branch, factor_branch, (vec_tile, dense_tile, left_tile, right_tile)
    )


def on_device(
    shear_stress,
    state_var,
    a_param,
    rate_param,
    loading,
    dense_tiles,
    left_factor,
    right_factor,
    admissible,
    tile_ranks,
):
    row_count = lax.axis_size("row")
    col_count = lax.axis_size("col")
    row_index = lax.axis_index("row")
    col_index = lax.axis_index("col")
    scenarios, piece_len = shear_stress.shape
    group_len = row_count // col_count
    tiles_down = dense_tiles.shape[0] // TILE
    tiles_across = dense_tiles.shape[1] // TILE

    def source_block(rounded):
        sub_width = piece_len // row_count
        pieces = rounded.reshape(scenarios, row_count, sub_width)
        moved = lax.all_to_all(
            lax.all_to_all(pieces, "row", split_axis=1, concat_axis=1, tiled=True),
            "col",
            split_axis=1,
            concat_axis=1,
            tiled=True,
        )
        gathered = lax.all_gather(moved, "row", axis=2, tiled=True)
        gathered = gathered.reshape(scenarios, col_count, group_len, piece_len)
        return jnp.transpose(gathered, (0, 2, 1, 3)).reshape(
            scenarios, group_len * col_count * piece_len
        )

    def local_product(source_vec):
        accum_sum = jnp.zeros((scenarios, TILE), jnp.float32)
        for tile_col in range(tiles_across):
            global_row = row_index * tiles_down + 0
            global_col = col_index * tiles_across + tile_col
            vec_tile = source_vec[:, tile_col * TILE : (tile_col + 1) * TILE]
            dense_tile = dense_tiles[0:TILE, tile_col * TILE : (tile_col + 1) * TILE]
            left_tile = left_factor[tile_col * RANK : (tile_col + 1) * RANK, 0:TILE]
            right_tile = right_factor[0:RANK, tile_col * TILE : (tile_col + 1) * TILE]
            accum_sum = accum_sum + tile_product(
                vec_tile,
                dense_tile,
                left_tile,
                right_tile,
                admissible[global_row, global_col],
                tile_ranks[global_row, global_col],
            )
        return accum_sum

    def rates(shear_now, state_now):
        velocity = slip_velocity(shear_now, state_now, a_param)
        rounded = velocity.astype(jnp.bfloat16)
        source_vec = source_block(rounded)
        partial_sum = local_product(source_vec)
        pushed = lax.psum_scatter(partial_sum, "col", scatter_dimension=1, tiled=True)
        k_shear = loading[None, :] - pushed
        k_state = rate_param[None, :] * (jnp.exp(-state_now) - jnp.abs(velocity))
        return (k_shear, k_state)

    k_shear1, k_state1 = rates(shear_stress, state_var)
    shear_mid = shear_stress + 0.5 * k_shear1
    state_mid = state_var + 0.5 * k_state1
    k_shear2, k_state2 = rates(shear_mid, state_mid)
    shear_next = shear_stress + 0.25 * (k_shear1 + k_shear2)
    state_next = state_var + 0.25 * (k_state1 + k_state2)
    return (shear_next, state_next)


def solution(mesh):
    placed = (
        P(None, ("row", "col")),
        P(None, ("row", "col")),
        P(("row", "col")),
        P(("row", "col")),
        P(("row", "col")),
        P("row", "col"),
        P("col", "row"),
        P("row", "col"),
        P(),
        P(),
    )
    return jax.shard_map(
        on_device,
        mesh=mesh,
        in_specs=placed,
        out_specs=(P(None, ("row", "col")), P(None, ("row", "col"))),
        check_vma=False,
    )
```

profile of v0, /device:TPU:0, one launch (start us, length us, event | category | flops | bytes accessed | tf_op | source)
XLA Modules:
  0.0 408.1 jit_solution(17271045453835936665)
XLA Ops:
  7.2 0.0 copy-start.6
  7.2 0.0 all-gather.3.cloned.1.call-start
  7.2 1.6 copy.24
  8.8 1.6 copy.15
  10.4 1.0 fusion.26
  11.4 14.7 %all_to_all.20 = bf16[512,8,64]{0,2,1:T(8,128)(2,1)S(1)} all-to-all(bf16[512,8,64]{0,2,1:T(8,128)(2,1)S(1)} %bitcast.35), channel_id=1, replica_groups=mesh['row'=8,'col'=4] {'row'}, dimensions={1} | all-to-all | bytes 1048576 | tf_op jit(solution)/shard_map/all_to_all | solution.py:61
  26.1 18.7 %all_to_all.21 = bf16[512,8,64]{0,2,1:T(8,128)(2,1)} all-to-all(bf16[512,8,64]{0,2,1:T(8,128)(2,1)S(1)} %all_to_all.20), channel_id=1, replica_groups=mesh['row'=8,'col'=4] {'col'}, dimensions={1} | all-to-all | bytes 1048576 | tf_op jit(solution)/shard_map/all_to_all | solution.py:60
  44.8 0.0 all-gather.3.cloned.1.call-update
  44.8 0.0 reduce-scatter.3.cloned.1.call-start
  44.9 1.4 fusion.33
  47.6 1.3 fusion.31
  48.8 0.0 copy-start.2
  48.9 12.4 %fusion.28 = (bf16[2048,2048]{1,0:T(8,128)(2,1)}, bf16[2048,2048]{1,0:T(8,128)(2,1)}) fusion(bf16[2048,4096]{1,0:T(8,128)(2,1)} %param.23), kind=kLoop, calls=%fused_computation.44 | loop fusion | bytes 33554432 | tf_op jit(solution)/shard_map/slice | solution.py:79
  61.3 18.1 %all-gather.3.cloned.1.call-done = bf16[512,8,512]{0,2,1:T(8,128)(2,1)} async-done(((bf16[512,8,64]{0,2,1:T(8,128)(2,1)}), bf16[512,8,512]{0,2,1:T(8,128)(2,1)}) %all-gather.3.cloned.1.call-update) | async-done | bytes 4194320 | tf_op jit(solution)/shard_map/all_gather | solution.py:67
  79.4 8.1 %copy.16 = bf16[512,2,4,512]{3,2,1,0:T(4,128)(2,1)} copy(bf16[512,2,4,512]{0,3,1,2:T(8,128)(2,1)} %bitcast.32) | data formatting | bytes 8388608 | tf_op jit(solution)/shard_map/transpose | solution.py:69
  87.5 7.7 %reshape.55 = bf16[512,4096]{1,0:T(8,128)(2,1)} reshape(bf16[512,2,4,512]{3,2,1,0:T(4,128)(2,1)} %copy.16) | data formatting | bytes 8388608 | tf_op jit(solution)/shard_map/reshape | solution.py:69
  95.3 4.8 %fusion.30 = (bf16[512,2048]{1,0:T(8,128)(2,1)}, bf16[512,2048]{1,0:T(8,128)(2,1)}) fusion(bf16[512,4096]{1,0:T(8,128)(2,1)} %reshape.55), kind=kLoop, calls=%fused_computation.46 | loop fusion | bytes 8388608 | tf_op jit(solution)/shard_map/slice | solution.py:78
  100.1 0.0 copy-done.2
  100.1 10.6 %conditional.4 = (f32[512,2048]{0,1:T(8,128)}) conditional(s32[]{:T(128)} %bitcast, (s32[]{:T(128)}, bf16[512,2048]{1,0:T(8,128)(2,1)}, bf16[64,2048]{1,0:T(8,128)(2,1)S(1)}, bf16[64,2048]{1,0:T(8,128)(2,1)S(1)}) %tuple.32, (bf16[512,2048]{1,0:T(8,128)(2,1)}, bf16[2048,2048]{1,0:T(8,128)(2,1)}) %tuple.33), branch_computations={%region_0.1_spmd, %region_1.2_spmd} | conditional | flops 4294967296 | bytes 14680072 | solution.py:31
  100.1 10.6 %fusion.35 = f32[512,2048]{0,1:T(8,128)} fusion(bf16[512,2048]{1,0:T(8,128)(2,1)} %get-tuple-element.64, bf16[2048,2048]{1,0:T(8,128)(2,1)} %get-tuple-element.65), kind=kOutput, calls=%fused_computation.51 | convolution fusion | flops 4294967296 | bytes 14680064 | tf_op jit(solution)/shard_map/cond | solution.py:31
  110.7 10.6 %conditional.5 = (f32[512,2048]{0,1:T(8,128)}) conditional(s32[]{:T(128)} %bitcast.5, (s32[]{:T(128)}, bf16[512,2048]{1,0:T(8,128)(2,1)}, bf16[64,2048]{1,0:T(8,128)(2,1)S(1)}, bf16[64,2048]{1,0:T(8,128)(2,1)S(1)}) %tuple.34, (bf16[512,2048]{1,0:T(8,128)(2,1)}, bf16[2048,2048]{1,0:T(8,128)(2,1)}) %tuple.35), branch_computations={%region_2.3_spmd, %region_3.4_spmd} | conditional | flops 4294967296 | bytes 14680072 | solution.py:31
  110.7 10.6 %fusion.36 = f32[512,2048]{0,1:T(8,128)} fusion(bf16[512,2048]{1,0:T(8,128)(2,1)} %get-tuple-element.70, bf16[2048,2048]{1,0:T(8,128)(2,1)} %get-tuple-element.71), kind=kOutput, calls=%fused_computation.52 | convolution fusion | flops 4294967296 | bytes 14680064 | tf_op jit(solution)/shard_map/cond | solution.py:31
  121.3 6.4 %add.60 = f32[512,2048]{0,1:T(8,128)} add(f32[512,2048]{0,1:T(8,128)} %get-tuple-element.88, f32[512,2048]{0,1:T(8,128)} %get-tuple-element.89) | non-fusion elementwise | flops 1048576 | bytes 12582912 | tf_op jit(solution)/shard_map/add | solution.py:82
  127.7 0.0 reduce-scatter.3.cloned.1.call-update
  127.7 0.0 all-gather.5.cloned.1.call-start
  127.8 76.9 %reduce-scatter.3.cloned.1.call-done = f32[512,512]{0,1:T(8,128)} async-done(((f32[512,2048]{0,1:T(8,128)}), f32[512,512]{0,1:T(8,128)}) %reduce-scatter.3.cloned.1.call-update) | async-done | bytes 1048592 | tf_op jit(solution)/shard_map/reduce_scatter | solution.py:97
  204.7 0.0 copy-done.7
  204.7 4.9 %multiply_add_fusion = (f32[512,512]{0,1:T(8,128)}, bf16[512,512]{0,1:T(8,128)(2,1)S(1)}) fusion(f32[512,512]{0,1:T(8,128)S(1)} %copy.15, f32[512]{0:T(512)S(1)} %copy-done.7, f32[512,512]{0,1:T(8,128)S(1)} %copy.24, f32[512]{0:T(512)S(1)} %copy-done.6, f32[512,512]{0,1:T(8,128)} %reduce-scatter.3.cloned.1.call-done, f32[512]{0:T(512)S(1)} %copy-done.5), kind=kLoop, calls=%fused_computation.36 | loop fusion | flops 10747904 | bytes 4724736 | tf_op jit(solution)/shard_map/add | solution.py:107
  209.6 13.2 %all_to_all.22 = bf16[512,8,64]{0,2,1:T(8,128)(2,1)S(1)} all-to-all(bf16[512,8,64]{0,2,1:T(8,128)(2,1)S(1)} %bitcast.34), channel_id=1, replica_groups=mesh['row'=8,'col'=4] {'row'}, dimensions={1} | all-to-all | bytes 1048576 | tf_op jit(solution)/shard_map/all_to_all | solution.py:61
  222.8 18.0 %all_to_all.23 = bf16[512,8,64]{0,2,1:T(8,128)(2,1)} all-to-all(bf16[512,8,64]{0,2,1:T(8,128)(2,1)S(1)} %all_to_all.22), channel_id=1, replica_groups=mesh['row'=8,'col'=4] {'col'}, dimensions={1} | all-to-all | bytes 1048576 | tf_op jit(solution)/shard_map/all_to_all | solution.py:60
  240.8 0.0 all-gather.5.cloned.1.call-update
  240.8 0.0 reduce-scatter.5.cloned.1.call-start
  240.9 34.5 %all-gather.5.cloned.1.call-done = bf16[512,8,512]{0,2,1:T(8,128)(2,1)} async-done(((bf16[512,8,64]{0,2,1:T(8,128)(2,1)}), bf16[512,8,512]{0,2,1:T(8,128)(2,1)}) %all-gather.5.cloned.1.call-update) | async-done | bytes 4194320 | tf_op jit(solution)/shard_map/all_gather | solution.py:67
  275.4 8.1 %copy.21 = bf16[512,2,4,512]{3,2,1,0:T(4,128)(2,1)} copy(bf16[512,2,4,512]{0,3,1,2:T(8,128)(2,1)} %bitcast.33) | data formatting | bytes 8388608 | tf_op jit(solution)/shard_map/transpose | solution.py:69
  283.5 7.7 %reshape.58 = bf16[512,4096]{1,0:T(8,128)(2,1)} reshape(bf16[512,2,4,512]{3,2,1,0:T(4,128)(2,1)} %copy.21) | data formatting | bytes 8388608 | tf_op jit(solution)/shard_map/reshape | solution.py:69
  291.2 4.0 fusion.29
  295.3 10.5 %conditional.7 = (f32[512,2048]{0,1:T(8,128)}) conditional(s32[]{:T(128)} %bitcast.5, (s32[]{:T(128)}, bf16[512,2048]{1,0:T(8,128)(2,1)}, bf16[64,2048]{1,0:T(8,128)(2,1)}, bf16[64,2048]{1,0:T(8,128)(2,1)}) %tuple.81, (bf16[512,2048]{1,0:T(8,128)(2,1)}, bf16[2048,2048]{1,0:T(8,128)(2,1)}) %tuple.39), branch_computations={%region_7.8_spmd, %region_8.9_spmd} | conditional | flops 4294967296 | bytes 14680072 | solution.py:31
  295.3 10.5 %fusion.38 = f32[512,2048]{0,1:T(8,128)} fusion(bf16[512,2048]{1,0:T(8,128)(2,1)} %get-tuple-element.82, bf16[2048,2048]{1,0:T(8,128)(2,1)} %get-tuple-element.83), kind=kOutput, calls=%fused_computation.54 | convolution fusion | flops 4294967296 | bytes 14680064 | tf_op jit(solution)/shard_map/cond | solution.py:31
  305.8 9.5 %conditional.6 = (f32[512,2048]{0,1:T(8,128)}) conditional(s32[]{:T(128)} %bitcast, (s32[]{:T(128)}, bf16[512,2048]{1,0:T(8,128)(2,1)S(1)}, bf16[64,2048]{1,0:T(8,128)(2,1)}, bf16[64,2048]{1,0:T(8,128)(2,1)S(1)}) %tuple.79, (bf16[512,2048]{1,0:T(8,128)(2,1)S(1)}, bf16[2048,2048]{1,0:T(8,128)(2,1)}) %tuple.37), branch_computations={%region_5.6_spmd, %region_6.7_spmd} | conditional | flops 4294967296 | bytes 14680072 | solution.py:31
  305.8 9.5 %fusion.37 = f32[512,2048]{0,1:T(8,128)} fusion(bf16[512,2048]{1,0:T(8,128)(2,1)S(1)} %get-tuple-element.76, bf16[2048,2048]{1,0:T(8,128)(2,1)} %get-tuple-element.77), kind=kOutput, calls=%fused_computation.53 | convolution fusion | flops 4294967296 | bytes 14680064 | tf_op jit(solution)/shard_map/cond | solution.py:31
  315.4 6.4 %add.63 = f32[512,2048]{0,1:T(8,128)} add(f32[512,2048]{0,1:T(8,128)} %get-tuple-element.90, f32[512,2048]{0,1:T(8,128)} %get-tuple-element.91) | non-fusion elementwise | flops 1048576 | bytes 12582912 | tf_op jit(solution)/shard_map/add | solution.py:82
  321.8 0.0 reduce-scatter.5.cloned.1.call-update
  321.8 1.2 copy-done
  323.0 1.3 copy.27
  324.3 74.4 %reduce-scatter.5.cloned.1.call-done = f32[512,512]{0,1:T(8,128)} async-done(((f32[512,2048]{0,1:T(8,128)}), f32[512,512]{0,1:T(8,128)}) %reduce-scatter.5.cloned.1.call-update) | async-done | bytes 1048592 | tf_op jit(solution)/shard_map/reduce_scatter | solution.py:97
  398.7 0.0 copy-done.1
  398.8 1.5 multiply_add_fusion.1
  400.2 1.3 copy.26
  (10 shorter events, 0.0 us)
Async XLA Ops:
  7.2 3.2 copy-start.6
  7.2 72.2 %all-gather.3.cloned.1.call-start = ((), (), s32[]{:S(2)}) async-start(), calls=%async_computation.6 | async-start | bytes 4718592 | tf_op jit(solution)/shard_map/all_gather | solution.py:67
  44.8 159.8 %reduce-scatter.3.cloned.1.call-start = ((), (), s32[]{:S(2)}) async-start(), calls=%async_computation.7 | async-start | bytes 5242880 | tf_op jit(solution)/shard_map/reduce_scatter | solution.py:97
  48.8 51.2 %copy-start.2 = (bf16[64,2048]{1,0:T(8,128)(2,1)}, bf16[64,2048]{1,0:T(8,128)(2,1)S(1)}, u32[]{:S(2)}) copy-start(bf16[64,2048]{1,0:T(8,128)(2,1)S(1)} %get-tuple-element.110) | copy-start | bytes 786436
  48.9 61.8 %copy-start.3 = (bf16[64,2048]{1,0:T(8,128)(2,1)}, bf16[64,2048]{1,0:T(8,128)(2,1)S(1)}, u32[]{:S(2)}) copy-start(bf16[64,2048]{1,0:T(8,128)(2,1)S(1)} %get-tuple-element.100) | copy-start | bytes 786436
  48.9 61.8 %copy-start.4 = (bf16[64,2048]{1,0:T(8,128)(2,1)}, bf16[64,2048]{1,0:T(8,128)(2,1)S(1)}, u32[]{:S(2)}) copy-start(bf16[64,2048]{1,0:T(8,128)(2,1)S(1)} %get-tuple-element.111) | copy-start | bytes 786436
  127.7 77.0 %copy-start.5 = (f32[512]{0:T(512)S(1)}, f32[512]{0:T(512)}, u32[]{:S(2)}) copy-start(f32[512]{0:T(512)} %param.22) | copy-start | bytes 6148
  127.7 77.0 %copy-start.7 = (f32[512]{0:T(512)S(1)}, f32[512]{0:T(512)}, u32[]{:S(2)}) copy-start(f32[512]{0:T(512)} %param.21) | copy-start | bytes 6148
  127.7 147.7 %all-gather.5.cloned.1.call-start = ((), (), s32[]{:S(2)}) async-start(), calls=%async_computation.8 | async-start | bytes 4718592 | tf_op jit(solution)/shard_map/all_gather | solution.py:67
  240.8 157.9 %reduce-scatter.5.cloned.1.call-start = ((), (), s32[]{:S(2)}) async-start(), calls=%async_computation.9 | async-start | bytes 5242880 | tf_op jit(solution)/shard_map/reduce_scatter | solution.py:97
  321.8 1.2 copy-start
  321.8 77.0 %copy-start.1 = (f32[512,512]{0,1:T(8,128)S(1)}, f32[512,512]{0,1:T(8,128)}, u32[]{:S(2)}) copy-start(f32[512,512]{0,1:T(8,128)} %reduce-scatter.3.cloned.1.call-done) | copy-start | bytes 3145732
Sparse Core Ops, SparseCore 0:
  45.0 34.4 all-gather.2
  127.9 76.7 reduce-scatter.2
  240.9 34.4 all-gather.4
  321.9 76.7 reduce-scatter.4
where the time goes:
time: 409 us; the launch traced here: 408 us
  waiting for transfers between devices  204 us (50%)
  blocking collectives  64.6 us (16%)
  local copies, waits for them, and re-layouts  62.6 us (15%)
  matrix products  41.2 us (10%)
  other arithmetic  20.3 us (5%)
  between operations  15.2 us (4%)
    reduce_scatter x2, waiting for transfers between devices, rates(): lax.psum_scatter(partial_sum, 'col', scatter_dimension=1, tiled=True)  151 us
    all_gather x2, waiting for transfers between devices, source_block(): gathered = lax.all_gather(moved, 'row', axis=2, tiled=True)  52.6 us
    cond x4, matrix products, tile_product(): lax.cond(is_dense == 1, dense_branch, factor_branch, (vec_tile, dense_til...  41.2 us
    all_to_all x2, blocking collectives, source_block(): lax.all_to_all(lax.all_to_all(pieces, 'row', split_axis=1, concat_axis=1,...  36.7 us
    all_to_all x2, blocking collectives, source_block(): lax.all_to_all(pieces, 'row', split_axis=1, concat_axis=1, tiled=True)  27.9 us
    transpose x2, local copies, waits for them, and re-layouts, source_block(): jnp.transpose(gathered, (0, 2, 1, 3))  16.2 us
    reshape x2, local copies, waits for them, and re-layouts, source_block(): jnp.transpose(gathered, (0, 2, 1, 3))  15.5 us
    add x2, other arithmetic, local_product(): accum_sum + tile_product(vec_tile, dense_tile, left_tile, right_tile, adm...  12.9 us
  transfers between devices with their start and end apart: 4, of which 4 were waited for; matrix products, arithmetic and copies ran while one was open for 4% of the time, Pallas kernels for 0%

commit v1 on v0

v1 whole, which is shorter than its diff:
```python
import functools
import math

import jax
import jax.numpy as jnp
from jax import lax
from jax.experimental import pallas as pl
from jax.experimental.pallas import tpu as pltpu
from jax.sharding import PartitionSpec as P

TILE = 2048
RANK = 64
GROUP = 16
LAG = 4
LN2 = math.log(2.0)
MESH = pl.DeviceIdType.MESH
F32 = jnp.float32
BF16 = jnp.bfloat16


def kernel(
    rows,
    cols,
    shear_ref,
    state_ref,
    a_ref,
    rate_ref,
    load_ref,
    dense_ref,
    left_ref,
    right_ref,
    adm_ref,
    rank_ref,
    shear_out,
    state_out,
    weights,
    gathered,
    vsend,
    psend,
    precv,
    own,
    k_shear,
    k_state,
    masked,
    dense_sem,
    p1_send,
    p1_recv,
    p2_send,
    fwd_send,
    p2_recv,
    rs_send,
    rs_recv,
):
    scenarios, piece = shear_ref.shape
    chunk = rows * GROUP
    chunks = scenarios // chunk
    gap = max(0, LAG - chunks)
    half = rows // 2
    per = rows // cols
    r = lax.axis_index("row")
    c = lax.axis_index("col")
    block = r // per
    slot = (r % per) * cols + c
    sib = r + 1 - 2 * (r % 2)
    targets, sources = weights.shape
    across = sources // TILE
    down = targets // TILE

    dense_copy = pltpu.make_async_copy(dense_ref, weights, dense_sem)

    def scen(q):
        return pl.ds(pl.multiple_of(q * chunk, chunk), chunk)

    def group_of(u, g):
        return gathered.at[u, pl.ds(pl.multiple_of(g * GROUP, GROUP), GROUP), :]

    def p1_copy(u, j):
        return pltpu.make_async_remote_copy(
            src_ref=vsend.at[u, pl.ds(pl.multiple_of(j * GROUP, GROUP), GROUP), :],
            dst_ref=gathered.at[
                u,
                pl.ds(pl.multiple_of(j * GROUP, GROUP), GROUP),
                pl.ds(pl.multiple_of(slot * piece, piece), piece),
            ],
            send_sem=p1_send.at[u, j],
            recv_sem=p1_recv.at[u],
            device_id=(j, block),
            device_id_type=MESH,
        )

    def p1_here(u, j):
        return pltpu.make_async_copy(
            vsend.at[u, pl.ds(pl.multiple_of(j * GROUP, GROUP), GROUP), :],
            gathered.at[
                u,
                pl.ds(pl.multiple_of(j * GROUP, GROUP), GROUP),
                pl.ds(pl.multiple_of(slot * piece, piece), piece),
            ],
            p1_recv.at[u],
        )

    def group_copy(u, g, send_sem, row_to):
        return pltpu.make_async_remote_copy(
            src_ref=group_of(u, g),
            dst_ref=group_of(u, g),
            send_sem=send_sem,
            recv_sem=p2_recv.at[u, g],
            device_id=(row_to, c),
            device_id_type=MESH,
        )

    def rs_copy(u, z):
        return pltpu.make_async_remote_copy(
            src_ref=psend.at[u, z],
            dst_ref=precv.at[u, c],
            send_sem=rs_send.at[u, z],
            recv_sem=rs_recv.at[u, c],
            device_id=(r, z),
            device_id_type=MESH,
        )

    def rs_arrival(u, z):
        return pltpu.make_async_remote_copy(
            src_ref=psend.at[u, z],
            dst_ref=precv.at[u, z],
            send_sem=rs_send.at[u, z],
            recv_sem=rs_recv.at[u, z],
            device_id=(r, z),
            device_id_type=MESH,
        )

    def velocity(shear_now, state_now):
        x = shear_now / a_ref[...]
        fade = jnp.exp(-state_now)
        v = (jnp.exp(x - LN2) - jnp.exp(-x - LN2)) * fade
        return v, rate_ref[...] * (fade - jnp.abs(v))

    def send_slip(u):
        def one(i, _):
            j = (r + 1 + i) % rows
            here = (j == r) & (block == c)

            @pl.when(here)
            def _():
                p1_here(u, j).start()

            @pl.when(jnp.logical_not(here))
            def _():
                p1_copy(u, j).start()

            return 0

        lax.fori_loop(0, rows, one, 0)

    def first_slip(q, _):
        v, ks = velocity(shear_ref[scen(q), :], state_ref[scen(q), :])
        vsend[q] = v.astype(BF16)
        k_state[scen(q), :] = ks
        send_slip(q)
        return 0

    def spread(u):
        pltpu.make_async_copy(group_of(u, r), group_of(u, r), p1_recv.at[u]).wait()
        group_copy(u, r, p2_send.at[u, half - 1], sib).start()

        def one(i, _):
            group_copy(u, r, p2_send.at[u, i], (r + 2 * (i + 1)) % rows).start()
            return 0

        lax.fori_loop(0, half - 1, one, 0)

    def forward(u):
        def one(i, _):
            g = (r + 2 * (i + 1)) % rows
            group_copy(u, g, fwd_send.at[u, i], sib).wait_recv()
            group_copy(u, g, fwd_send.at[u, i], sib).start()
            return 0

        lax.fori_loop(0, half - 1, one, 0)

    def multiply(u):
        def arrive(i, _):
            group_copy(u, (sib + 2 * i) % rows, p1_send.at[u, 0], sib).wait_recv()
            return 0

        lax.fori_loop(0, half, arrive, 0)

        def one(i, _):
            z = (c + 1 + i) % cols
            part = lax.dot_general(
                gathered[u],
                weights[pl.ds(pl.multiple_of(z * piece, piece), piece), :],
                (((1,), (1,)), ((), ())),
                preferred_element_type=F32,
            )

            @pl.when(i < cols - 1)
            def _():
                psend[u, z] = part.astype(BF16)
                rs_copy(u, z).start()

            @pl.when(i == cols - 1)
            def _():
                own[u] = part

            return 0

        lax.fori_loop(0, cols, one, 0)

    def finish(u):
        def one(i, _):
            z = (c + 1 + i) % cols
            rs_arrival(u, z).wait_recv()
            own[u] = own[u] + precv[u, z].astype(F32)
            return 0

        lax.fori_loop(0, cols - 1, one, 0)

        @pl.when(u < chunks)
        def _():
            here = scen(u)
            ks = load_ref[...] - own[u]
            k_shear[here, :] = ks
            k1 = k_state[here, :]
            state = state_ref[here, :]
            v, k2 = velocity(shear_ref[here, :] + 0.5 * ks, state + 0.5 * k1)
            vsend[u + chunks] = v.astype(BF16)
            send_slip(u + chunks)
            state_out[here, :] = state + 0.25 * (k1 + k2)

        @pl.when(u >= chunks)
        def _():
            here = scen(u - chunks)
            ks = load_ref[...] - own[u]
            shear_out[here, :] = shear_ref[here, :] + 0.25 * (k_shear[here, :] + ks)

    build_rows = 256
    builds = targets // build_rows
    build_cols = 512

    def build(b, _):
        start = pl.multiple_of(b * build_rows, build_rows)
        here = pl.ds(start, build_rows)
        td = (b * build_rows) // TILE
        for k in range(across):
            dense = adm_ref[r * down + td, c * across + k]
            rank = rank_ref[r * down + td, c * across + k]
            left = left_ref[k * RANK : (k + 1) * RANK, here]
            keep = lax.broadcasted_iota(jnp.int32, (RANK, build_rows), 0) < rank
            left = jnp.where(keep, left.astype(F32), 0.0)
            left = jnp.transpose(left).astype(BF16)
            for s in range(TILE // build_cols):
                span = slice(k * TILE + s * build_cols, k * TILE + (s + 1) * build_cols)
                right = right_ref[pl.ds(pl.multiple_of(td * RANK, RANK), RANK), span]
                term = jnp.dot(left, right, preferred_element_type=F32)
                is_dense = jnp.full(term.shape, dense, jnp.int32) == 1
                weights[here, span] = jnp.where(
                    is_dense, weights[here, span].astype(F32), term
                ).astype(BF16)
        return 0

    dense_copy.start()
    lax.fori_loop(0, chunks, first_slip, 0)

    def at_slot(sigma, body):
        valid = ((sigma >= 0) & (sigma < chunks)) | (
            (sigma >= chunks + gap) & (sigma < 2 * chunks + gap)
        )
        u = jnp.where(sigma < chunks, sigma, sigma - gap)

        @pl.when(valid)
        def _():
            body(u)

    def step(t, _):
        at_slot(t, spread)
        at_slot(t - 1, forward)

        @pl.when(t == 0)
        def _():
            dense_copy.wait()

        @pl.when(t < 2)
        def _():
            lax.fori_loop(t * builds // 2, (t + 1) * builds // 2, build, 0)

        at_slot(t - 2, multiply)
        at_slot(t - 3, finish)
        return 0

    lax.fori_loop(0, 2 * chunks + gap + 3, step, 0)

    def drain(u, _):
        def p1(j, _):
            @pl.when(jnp.logical_not((j == r) & (block == c)))
            def _():
                p1_copy(u, j).wait_send()

            return 0

        lax.fori_loop(0, rows, p1, 0)

        def p2(i, _):
            group_copy(u, r, p2_send.at[u, i], sib).wait_send()
            return 0

        lax.fori_loop(0, half, p2, 0)

        def fwd(i, _):
            group_copy(u, r, fwd_send.at[u, i], sib).wait_send()
            return 0

        lax.fori_loop(0, half - 1, fwd, 0)

        def rs(i, _):
            rs_copy(u, (c + 1 + i) % cols).wait_send()
            return 0

        lax.fori_loop(0, cols - 1, rs, 0)
        return 0

    lax.fori_loop(0, 2 * chunks, drain, 0)


def solution(mesh):
    rows, cols = mesh.shape["row"], mesh.shape["col"]

    def on_device(
        shear, state, a_param, rate, loading, dense, left, right, admissible, ranks
    ):
        scenarios, piece = shear.shape
        chunk = rows * GROUP
        units = 2 * (scenarios // chunk)
        vmem = pl.BlockSpec(memory_space=pltpu.VMEM)
        smem = pl.BlockSpec(memory_space=pltpu.SMEM)
        hbm = pl.BlockSpec(memory_space=pl.ANY)
        dma = pltpu.SemaphoreType.DMA
        return pl.pallas_call(
            functools.partial(kernel, rows, cols),
            out_shape=(
                jax.ShapeDtypeStruct(shear.shape, F32),
                jax.ShapeDtypeStruct(shear.shape, F32),
            ),
            in_specs=[vmem] * 5 + [hbm, vmem, vmem, smem, smem],
            out_specs=(vmem, vmem),
            scratch_shapes=[
                pltpu.VMEM(dense.shape, BF16),
                pltpu.VMEM((units, chunk, dense.shape[1]), BF16),
                pltpu.VMEM((units, chunk, piece), BF16),
                pltpu.VMEM((units, cols, chunk, piece), BF16),
                pltpu.VMEM((units, cols, chunk, piece), BF16),
                pltpu.VMEM((units, chunk, piece), F32),
                pltpu.VMEM(shear.shape, F32),
                pltpu.VMEM(shear.shape, F32),
                pltpu.VMEM((8, 128), F32),
                dma,
                dma((units, rows)),
                dma((units,)),
                dma((units, rows // 2)),
                dma((units, rows // 2)),
                dma((units, rows)),
                dma((units, cols)),
                dma((units, cols)),
            ],
            compiler_params=pltpu.CompilerParams(
                has_side_effects=True, vmem_limit_bytes=62 * 1024 * 1024
            ),
        )(
            shear,
            state,
            a_param[None, :],
            rate[None, :],
            loading[None, :],
            dense,
            left,
            right,
            admissible,
            ranks,
        )

    wide = P(None, ("row", "col"))
    line = P(("row", "col"))
    placed = (
        wide,
        wide,
        line,
        line,
        line,
        P("row", "col"),
        P("col", "row"),
        P("row", "col"),
        P(),
        P(),
    )
    return jax.shard_map(
        on_device, mesh=mesh, in_specs=placed, out_specs=(wide, wide), check_vma=False
    )
```

time: 409 us -> 187 us (0.46)
  waiting for transfers between devices: 204 us -> 0 us
  Pallas kernels: 0 us -> 181 us
  blocking collectives: 64.6 us -> 0 us
  local copies, waits for them, and re-layouts: 62.6 us -> 4.52 us
  matrix products: 41.2 us -> 0 us
  other arithmetic: 20.3 us -> 0 us
  between operations: 15.2 us -> 0.64 us
    pallas_call x0 -> x1, Pallas kernels: none -> 181 us  [on_device(): pl.pallas_call(functools.partial(kernel, rows, cols), out_shape=(jax.Shap...]
    reduce_scatter x2 -> x0, waiting for transfers between devices: 151 us -> none  [rates(): lax.psum_scatter(partial_sum, 'col', scatter_dimension=1, tiled=True)]
    all_to_all x4 -> x0, blocking collectives: 64.6 us -> none  [the longest x2 36.7 us: source_block(): lax.all_to_all(lax.all_to_all(pieces, 'row', split_axis=1, concat_axis=1,...]
    all_gather x2 -> x0, waiting for transfers between devices: 52.6 us -> none  [source_block(): gathered = lax.all_gather(moved, 'row', axis=2, tiled=True)]
    cond x4 -> x0, matrix products: 41.2 us -> none  [tile_product(): lax.cond(is_dense == 1, dense_branch, factor_branch, (vec_tile, dense_til...]
    slice x4 -> x0, local copies, waits for them, and re-layouts: 22.5 us -> none  [the longest x1 12.4 us: local_product(): dense_tile = dense_tiles[0:TILE, tile_col * TILE:(tile_col + 1) * TILE]]
    add x4 -> x0, other arithmetic: 19.3 us -> none  [the longest x2 12.9 us: local_product(): accum_sum + tile_product(vec_tile, dense_tile, left_tile, right_tile, adm...]
    transpose x2 -> x0, local copies, waits for them, and re-layouts: 16.2 us -> none  [source_block(): jnp.transpose(gathered, (0, 2, 1, 3))]
  transfers between devices with their start and end apart: 4 -> 0, of which waited for: 4 -> 0; matrix products, arithmetic and copies ran while one was open for 4% -> 0% of each run, Pallas kernels for 0% -> 0%
where the time goes in v1:
time: 187 us; the launch traced here: 186 us
  Pallas kernels  181 us (97%)
  local copies, waits for them, and re-layouts  4.52 us (2%)
    pallas_call x1, Pallas kernels, on_device(): pl.pallas_call(functools.partial(kernel, rows, cols), out_shape=(jax.Shap...  181 us
    unnamed x2, local copies, waits for them, and re-layouts  4.52 us

profile of v1, /device:TPU:0, one launch (start us, length us, event | category | flops | bytes accessed | tf_op | source)
XLA Modules:
  0.0 186.0 jit_solution(3552380543351762930)
XLA Ops:
  0.6 180.9 %shard_map.113 = (f32[512,512]{1,0:T(8,128)}, f32[512,512]{1,0:T(8,128)}) custom-call(f32[512,512]{1,0:T(8,128)} %shear_ref.1, f32[512,512]{1,0:T(8,128)} %state_ref.1, f32[1,512]{1,0:T(1,128)} %bitcast.3, f32[1,512]{1,0:T(1,128)} %bitcast.4, f32[1,512]{1,0:T(1,128)} %bitcast.5, bf16[2048,4096]{1,0:T(8,128)(2,1)} %dense_ref.1, bf16[128,2048]{1,0:T(8,128)(2,1)} %left_ref.1, ...), custom_call_target="tpu_custom_call" | custom-call | tf_op jit(solution)/shard_map/pallas_call | solution.py:338
  181.5 2.3 %copy.14 = f32[512,512]{1,0:T(8,128)} copy(f32[512,512]{1,0:T(8,128)} %get-tuple-element.4) | data formatting | bytes 2097152
  183.8 2.3 %copy.15 = f32[512,512]{1,0:T(8,128)} copy(f32[512,512]{1,0:T(8,128)} %get-tuple-element.5) | data formatting | bytes 2097152

commit v2 on v1

--- a/solution.py
+++ b/solution.py
@@ -36,13 +36,15 @@
     weights,
     gathered,
     vsend,
+    staged,
     psend,
     precv,
     own,
     k_shear,
     k_state,
-    masked,
     dense_sem,
+    st_send,
+    st_recv,
     p1_send,
     p1_recv,
     p2_send,
@@ -59,8 +61,7 @@
     per = rows // cols
     r = lax.axis_index("row")
     c = lax.axis_index("col")
-    block = r // per
-    slot = (r % per) * cols + c
+    mine = c * per
     sib = r + 1 - 2 * (r % 2)
     targets, sources = weights.shape
     across = sources // TILE
@@ -74,29 +75,35 @@
     def group_of(u, g):
         return gathered.at[u, pl.ds(pl.multiple_of(g * GROUP, GROUP), GROUP), :]
 
-    def p1_copy(u, j):
+    def part_of(u, g):
+        return vsend.at[u, pl.ds(pl.multiple_of(g * GROUP, GROUP), GROUP), :]
+
+    def st_copy(u, j):
         return pltpu.make_async_remote_copy(
-            src_ref=vsend.at[u, pl.ds(pl.multiple_of(j * GROUP, GROUP), GROUP), :],
-            dst_ref=gathered.at[
-                u,
-                pl.ds(pl.multiple_of(j * GROUP, GROUP), GROUP),
-                pl.ds(pl.multiple_of(slot * piece, piece), piece),
-            ],
-            send_sem=p1_send.at[u, j],
+            src_ref=part_of(u, j),
+            dst_ref=staged.at[u, r],
+            send_sem=st_send.at[u, j],
+            recv_sem=st_recv.at[u],
+            device_id=(j, c),
+            device_id_type=MESH,
+        )
+
+    def place(u, source):
+        slot = (source % per) * cols + c
+        return gathered.at[
+            u,
+            pl.ds(pl.multiple_of(r * GROUP, GROUP), GROUP),
+            pl.ds(pl.multiple_of(slot * piece, piece), piece),
+        ]
+
+    def p1_copy(u, source):
+        return pltpu.make_async_remote_copy(
+            src_ref=staged.at[u, source],
+            dst_ref=place(u, source),
+            send_sem=p1_send.at[u, source],
             recv_sem=p1_recv.at[u],
-            device_id=(j, block),
+            device_id=(r, source // per),
             device_id_type=MESH,
-        )
-
-    def p1_here(u, j):
-        return pltpu.make_async_copy(
-            vsend.at[u, pl.ds(pl.multiple_of(j * GROUP, GROUP), GROUP), :],
-            gathered.at[
-                u,
-                pl.ds(pl.multiple_of(j * GROUP, GROUP), GROUP),
-                pl.ds(pl.multiple_of(slot * piece, piece), piece),
-            ],
-            p1_recv.at[u],
         )
 
     def group_copy(u, g, send_sem, row_to):
@@ -137,20 +144,28 @@
 
     def send_slip(u):
         def one(i, _):
-            j = (r + 1 + i) % rows
-            here = (j == r) & (block == c)
-
-            @pl.when(here)
-            def _():
-                p1_here(u, j).start()
-
-            @pl.when(jnp.logical_not(here))
-            def _():
-                p1_copy(u, j).start()
-
-            return 0
-
-        lax.fori_loop(0, rows, one, 0)
+            st_copy(u, (r + 1 + i) % rows).start()
+            return 0
+
+        lax.fori_loop(0, rows - 1, one, 0)
+        pltpu.make_async_copy(part_of(u, r), staged.at[u, r], st_recv.at[u]).start()
+
+    def relay(u):
+        pltpu.make_async_copy(staged.at[u], staged.at[u], st_recv.at[u]).wait()
+
+        def one(i, _):
+            p1_copy(u, (mine + per + i) % rows).start()
+            return 0
+
+        lax.fori_loop(0, rows - per, one, 0)
+
+        def stay(i, _):
+            pltpu.make_async_copy(
+                staged.at[u, mine + i], place(u, mine + i), p1_recv.at[u]
+            ).start()
+            return 0
+
+        lax.fori_loop(0, per, stay, 0)
 
     def first_slip(q, _):
         v, ks = velocity(shear_ref[scen(q), :], state_ref[scen(q), :])
@@ -273,8 +288,10 @@
             body(u)
 
     def step(t, _):
+        at_slot(t - 1, forward)
+        at_slot(t, relay)
+        at_slot(t - 2, multiply)
         at_slot(t, spread)
-        at_slot(t - 1, forward)
 
         @pl.when(t == 0)
         def _():
@@ -284,21 +301,23 @@
         def _():
             lax.fori_loop(t * builds // 2, (t + 1) * builds // 2, build, 0)
 
-        at_slot(t - 2, multiply)
         at_slot(t - 3, finish)
         return 0
 
     lax.fori_loop(0, 2 * chunks + gap + 3, step, 0)
 
     def drain(u, _):
-        def p1(j, _):
-            @pl.when(jnp.logical_not((j == r) & (block == c)))
-            def _():
-                p1_copy(u, j).wait_send()
-
-            return 0
-
-        lax.fori_loop(0, rows, p1, 0)
+        def st(i, _):
+            st_copy(u, (r + 1 + i) % rows).wait_send()
+            return 0
+
+        lax.fori_loop(0, rows - 1, st, 0)
+
+        def p1(i, _):
+            p1_copy(u, (mine + per + i) % rows).wait_send()
+            return 0
+
+        lax.fori_loop(0, rows - per, p1, 0)
 
         def p2(i, _):
             group_copy(u, r, p2_send.at[u, i], sib).wait_send()
@@ -347,13 +366,15 @@
                 pltpu.VMEM(dense.shape, BF16),
                 pltpu.VMEM((units, chunk, dense.shape[1]), BF16),
                 pltpu.VMEM((units, chunk, piece), BF16),
+                pltpu.VMEM((units, rows, GROUP, piece), BF16),
                 pltpu.VMEM((units, cols, chunk, piece), BF16),
                 pltpu.VMEM((units, cols, chunk, piece), BF16),
                 pltpu.VMEM((units, chunk, piece), F32),
                 pltpu.VMEM(shear.shape, F32),
                 pltpu.VMEM(shear.shape, F32),
-                pltpu.VMEM((8, 128), F32),
                 dma,
+                dma((units, rows)),
+                dma((units,)),
                 dma((units, rows)),
                 dma((units,)),
                 dma((units, rows // 2)),

time: 187 us -> 165 us (0.88)
  Pallas kernels: 181 us -> 159 us
    pallas_call x1, Pallas kernels: 181 us -> 159 us  [on_device(): pl.pallas_call(functools.partial(kernel, rows, cols), out_shape=(jax.Shap...]
where the time goes in v2:
time: 165 us; the launch traced here: 164 us
  Pallas kernels  159 us (96%)
  local copies, waits for them, and re-layouts  4.52 us (3%)
    pallas_call x1, Pallas kernels, on_device(): pl.pallas_call(functools.partial(kernel, rows, cols), out_shape=(jax.Shap...  159 us
    unnamed x2, local copies, waits for them, and re-layouts  4.52 us

profile of v2, /device:TPU:0, one launch (start us, length us, event | category | flops | bytes accessed | tf_op | source)
XLA Modules:
  0.0 164.5 jit_solution(12283652888289401108)
XLA Ops:
  0.6 159.3 %shard_map.113 = (f32[512,512]{1,0:T(8,128)}, f32[512,512]{1,0:T(8,128)}) custom-call(f32[512,512]{1,0:T(8,128)} %shear_ref.1, f32[512,512]{1,0:T(8,128)} %state_ref.1, f32[1,512]{1,0:T(1,128)} %bitcast.3, f32[1,512]{1,0:T(1,128)} %bitcast.4, f32[1,512]{1,0:T(1,128)} %bitcast.5, bf16[2048,4096]{1,0:T(8,128)(2,1)} %dense_ref.1, bf16[128,2048]{1,0:T(8,128)(2,1)} %left_ref.1, ...), custom_call_target="tpu_custom_call" | custom-call | tf_op jit(solution)/shard_map/pallas_call | solution.py:357
  160.0 2.3 %copy.14 = f32[512,512]{1,0:T(8,128)} copy(f32[512,512]{1,0:T(8,128)} %get-tuple-element.4) | data formatting | bytes 2097152
  162.2 2.3 %copy.15 = f32[512,512]{1,0:T(8,128)} copy(f32[512,512]{1,0:T(8,128)} %get-tuple-element.5) | data formatting | bytes 2097152

commit v3 on v2

--- a/solution.py
+++ b/solution.py
@@ -277,6 +277,12 @@
     dense_copy.start()
     lax.fori_loop(0, chunks, first_slip, 0)
 
+    def first_relay(q, _):
+        relay(q)
+        return 0
+
+    lax.fori_loop(0, chunks, first_relay, 0)
+
     def at_slot(sigma, body):
         valid = ((sigma >= 0) & (sigma < chunks)) | (
             (sigma >= chunks + gap) & (sigma < 2 * chunks + gap)
@@ -288,9 +294,13 @@
             body(u)
 
     def step(t, _):
+        at_slot(t - 2, multiply)
+
+        @pl.when((t >= chunks + gap) & (t < 2 * chunks + gap))
+        def _():
+            relay(t - gap)
+
         at_slot(t - 1, forward)
-        at_slot(t, relay)
-        at_slot(t - 2, multiply)
         at_slot(t, spread)
 
         @pl.when(t == 0)

time: 165 us -> 159 us (0.964)
  Pallas kernels: 159 us -> 153 us
    pallas_call x1, Pallas kernels: 159 us -> 153 us  [on_device(): pl.pallas_call(functools.partial(kernel, rows, cols), out_shape=(jax.Shap...]
where the time goes in v3:
time: 159 us; the launch traced here: 158 us
  Pallas kernels  153 us (96%)
  local copies, waits for them, and re-layouts  4.52 us (3%)
    pallas_call x1, Pallas kernels, on_device(): pl.pallas_call(functools.partial(kernel, rows, cols), out_shape=(jax.Shap...  153 us
    unnamed x2, local copies, waits for them, and re-layouts  4.52 us

profile of v3, /device:TPU:0, one launch (start us, length us, event | category | flops | bytes accessed | tf_op | source)
XLA Modules:
  0.0 158.4 jit_solution(17296030060554413027)
XLA Ops:
  0.6 153.2 %shard_map.113 = (f32[512,512]{1,0:T(8,128)}, f32[512,512]{1,0:T(8,128)}) custom-call(f32[512,512]{1,0:T(8,128)} %shear_ref.1, f32[512,512]{1,0:T(8,128)} %state_ref.1, f32[1,512]{1,0:T(1,128)} %bitcast.3, f32[1,512]{1,0:T(1,128)} %bitcast.4, f32[1,512]{1,0:T(1,128)} %bitcast.5, bf16[2048,4096]{1,0:T(8,128)(2,1)} %dense_ref.1, bf16[128,2048]{1,0:T(8,128)(2,1)} %left_ref.1, ...), custom_call_target="tpu_custom_call" | custom-call | tf_op jit(solution)/shard_map/pallas_call | solution.py:367
  153.9 2.3 %copy.14 = f32[512,512]{1,0:T(8,128)} copy(f32[512,512]{1,0:T(8,128)} %get-tuple-element.4) | data formatting | bytes 2097152
  156.1 2.3 %copy.15 = f32[512,512]{1,0:T(8,128)} copy(f32[512,512]{1,0:T(8,128)} %get-tuple-element.5) | data formatting | bytes 2097152
